TPU v7x, 32 devices: a whole 2x2x4 slice. The times are simulated.
32 devices in a mesh: seq: 4 (over y, x), fsdp: 8 (over z, core).
Axes of the slice: x: 2, y: 2, z: 4, core: 2. Of those that a mesh axis runs over, the one named last changes fastest.
Arguments:
- tokens: bfloat16 [8, 1536, 1024], P('fsdp', 'seq'), may hold values from -6 to 6
- segment_ids: int32 [8, 1536], P('fsdp', 'seq'), may hold values from 0 to 5, never falling along the last dimension, each value on 1 to 768 neighbouring positions
- random_blocks: int32 [16, 22, 3], P('seq'), may hold values from 1 to 22, as said below
- ln1_gain: bfloat16 [1024], P('fsdp'), may hold values from 0.099609375 to 1.8984375
- ln1_bias: bfloat16 [1024], P('fsdp'), may hold values from -4 to 4
- w_qkv: bfloat16 [1024, 3072], P('fsdp'), may hold values from -0.25 to 0.25
- w_out: bfloat16 [1024, 1024], P('fsdp'), may hold values from -0.5 to 0.5
- ln2_gain: bfloat16 [1024], P('fsdp'), may hold values from 0.099609375 to 1.8984375
- ln2_bias: bfloat16 [1024], P('fsdp'), may hold values from -4 to 4
- w_in: bfloat16 [1024, 4096], P('fsdp'), may hold values from -0.1875 to 0.1875
- b_in: bfloat16 [4096], P('fsdp'), may hold values from -4 to 4
- w_down: bfloat16 [4096, 1024], P('fsdp'), may hold values from -0.09375 to 0.09375
- b_down: bfloat16 [1024], P('fsdp'), may hold values from -4 to 4
- cotangent: bfloat16 [8, 1536, 1024], P('fsdp', 'seq'), may hold values from -6 to 6
Outputs:
- output: bfloat16 [8, 1536, 1024], P('fsdp', 'seq')
- grad_tokens: bfloat16 [8, 1536, 1024], P('fsdp', 'seq')
- grad_ln1_gain: float32 [1024], P('fsdp')
- grad_ln1_bias: float32 [1024], P('fsdp')
- grad_qkv: float32 [1024, 3072], P('fsdp')
- grad_out_proj: float32 [1024, 1024], P('fsdp')
- grad_ln2_gain: float32 [1024], P('fsdp')
- grad_ln2_bias: float32 [1024], P('fsdp')
- grad_in: float32 [1024, 4096], P('fsdp')
- grad_in_bias: float32 [4096], P('fsdp')
- grad_down: float32 [4096, 1024], P('fsdp')
- grad_down_bias: float32 [1024], P('fsdp')
Inputs may be any that keep to these rules, and one draw needn't show every extreme that they name: For head h and query block b + 1, the 3 entries random_blocks[h, b, :] are different key blocks, none of them 0, 23, b, b + 1 or b + 2. `segment_ids`: in each sequence the segment numbers start at 0, never fall and take every value up to 5; a document has at most 768 tokens, and some document has exactly that many.
All inputs are finite; a program needn't handle non-finite values.
Results may differ from a plain program's by a relative error of at most 0.014.
Values may be sent and summed in bfloat16 or wider, within the bound.
A program may use at most 256 MiB of HBM per device.

v0:
```python
import math
import jax
import jax.numpy as jnp
from jax import lax
from jax.sharding import PartitionSpec as P

DH = 64
BLK = 64


def build_lists(random_blocks, blocks):
    middle_ids = jnp.arange(1, blocks - 1, dtype=jnp.int32)
    head_count = random_blocks.shape[0]
    window_ids = jnp.stack([middle_ids - 1, middle_ids, middle_ids + 1], axis=-1)
    global_ids = jnp.stack(
        [jnp.zeros_like(middle_ids), jnp.full_like(middle_ids, blocks - 1)], axis=-1
    )
    block_list = jnp.concatenate(
        [
            jnp.broadcast_to(window_ids, (head_count, blocks - 2, 3)),
            random_blocks,
            jnp.broadcast_to(global_ids, (head_count, blocks - 2, 2)),
        ],
        axis=-1,
    )
    usable = jnp.concatenate(
        [
            jnp.ones((blocks - 2, 3 + random_blocks.shape[2]), dtype=bool),
            (middle_ids != 1)[:, None],
            (middle_ids != blocks - 2)[:, None],
        ],
        axis=-1,
    )
    return (block_list, usable)


def masked_softmax(scores, allowed):
    shifted = jnp.where(allowed, scores, -1e30)
    top_score = jnp.max(shifted, axis=-1, keepdims=True)
    log_total = top_score + jnp.log(jnp.sum(jnp.exp(shifted - top_score), axis=-1, keepdims=True))
    return (jnp.exp(shifted - log_total), log_total)


def layer_norm(token_rows, gain_vec, bias_vec):
    center = token_rows - jnp.mean(token_rows, axis=-1, keepdims=True)
    variance = jnp.mean(center * center, axis=-1, keepdims=True)
    return center * lax.rsqrt(variance + 1e-05) * gain_vec + bias_vec


def gelu_tanh(pre_act):
    return (
        0.5
        * pre_act
        * (1.0 + jnp.tanh(0.7978845608028654 * (pre_act + 0.044715 * pre_act * pre_act * pre_act)))
    )


def lead_dot(left_arr, right_arr):
    return lax.dot_general(
        left_arr, right_arr, (((0,), (0,)), ((), ())), preferred_element_type=jnp.float32
    )


def last_dot(left_arr, right_arr):
    return lax.dot_general(
        left_arr, right_arr, (((1,), (1,)), ((), ())), preferred_element_type=jnp.float32
    )


def head_setup(queries, keys_all, values_all, block_list, usable, segments):
    length = queries.shape[0]
    blocks = length // BLK
    slot_count = block_list.shape[1]
    blocked_queries = queries.reshape(blocks, BLK, DH)
    neighbour_keys = keys_all.reshape(blocks, BLK, DH)[block_list].reshape(
        blocks - 2, slot_count * BLK, DH
    )
    neighbour_values = values_all.reshape(blocks, BLK, DH)[block_list].reshape(
        blocks - 2, slot_count * BLK, DH
    )
    seg_blocks = segments.reshape(blocks, BLK)
    key_seg = seg_blocks[block_list].reshape(blocks - 2, slot_count * BLK)
    allowed = (seg_blocks[1:-1][:, :, None] == key_seg[:, None, :]) & jnp.repeat(
        usable, BLK, axis=1
    )[:, None, :]
    edge_queries = jnp.concatenate([blocked_queries[0], blocked_queries[-1]], axis=0)
    edge_seg = jnp.concatenate([seg_blocks[0], seg_blocks[-1]], axis=0)
    edge_allowed = edge_seg[:, None] == segments[None, :]
    return (blocked_queries, neighbour_keys, neighbour_values, allowed, edge_queries, edge_allowed)


def head_forward(queries, keys_all, values_all, block_list, usable, segments):
    score_scale = 1.0 / math.sqrt(DH)
    blocked_queries, neighbour_keys, neighbour_values, allowed, edge_queries, edge_allowed = (
        head_setup(queries, keys_all, values_all, block_list, usable, segments)
    )
    unscaled_scores = jnp.einsum(
        "vfn,vmn->vfm", blocked_queries[1:-1], neighbour_keys, preferred_element_type=jnp.float32
    )
    middle_probability, log_mid = masked_softmax(unscaled_scores * score_scale, allowed)
    middle_output = jnp.einsum(
        "icf,ifl->icl",
        middle_probability.astype(jnp.bfloat16),
        neighbour_values,
        preferred_element_type=jnp.float32,
    )
    edge_raw = last_dot(edge_queries, keys_all)
    prob_edge, log_edge = masked_softmax(edge_raw * score_scale, edge_allowed)
    out_edge = jnp.dot(
        prob_edge.astype(jnp.bfloat16), values_all, preferred_element_type=jnp.float32
    )
    merged = jnp.concatenate(
        [out_edge[:BLK], middle_output.reshape(-1, DH), out_edge[BLK:]], axis=0
    )
    return (merged, log_mid, log_edge)


def head_backward(
    queries, keys_all, values_all, block_list, log_mid, log_edge, grad_out, usable, segments
):
    score_scale = 1.0 / math.sqrt(DH)
    length = queries.shape[0]
    blocks = length // BLK
    slot_count = block_list.shape[1]
    blocked_queries, neighbour_keys, neighbour_values, allowed, edge_queries, edge_allowed = (
        head_setup(queries, keys_all, values_all, block_list, usable, segments)
    )
    unscaled_scores = jnp.einsum(
        "vfn,vmn->vfm", blocked_queries[1:-1], neighbour_keys, preferred_element_type=jnp.float32
    )
    middle_probability = jnp.exp(jnp.where(allowed, unscaled_scores * score_scale, -1e30) - log_mid)
    middle_lower_precision = middle_probability.astype(jnp.bfloat16)
    grad_blocks = grad_out.reshape(blocks, BLK, DH)
    middle_block_gradient = grad_blocks[1:-1]
    grad_prob = jnp.einsum(
        "vfn,vmn->vfm", middle_block_gradient, neighbour_values, preferred_element_type=jnp.float32
    )
    delta_mid = jnp.sum(grad_prob * middle_probability, axis=-1, keepdims=True)
    score_gradient = (middle_probability * (grad_prob - delta_mid) * score_scale).astype(
        jnp.bfloat16
    )
    grad_query_mid = jnp.einsum(
        "icf,ifl->icl", score_gradient, neighbour_keys, preferred_element_type=jnp.float32
    )
    near_shape = (blocks - 2, slot_count, BLK, DH)
    grad_near_keys = jnp.einsum(
        "onm,ons->oms", score_gradient, blocked_queries[1:-1], preferred_element_type=jnp.float32
    ).reshape(near_shape)
    grad_near_values = jnp.einsum(
        "onm,ons->oms",
        middle_lower_precision,
        middle_block_gradient,
        preferred_element_type=jnp.float32,
    ).reshape(near_shape)
    edge_raw = last_dot(edge_queries, keys_all)
    prob_edge = jnp.exp(jnp.where(edge_allowed, edge_raw * score_scale, -1e30) - log_edge)
    edge_low = prob_edge.astype(jnp.bfloat16)
    grad_edge = jnp.concatenate([grad_blocks[0], grad_blocks[-1]], axis=0)
    grad_edge_prob = last_dot(grad_edge, values_all)
    delta_edge = jnp.sum(grad_edge_prob * prob_edge, axis=-1, keepdims=True)
    grad_edge_scores = (prob_edge * (grad_edge_prob - delta_edge) * score_scale).astype(
        jnp.bfloat16
    )
    grad_query_edge = jnp.dot(grad_edge_scores, keys_all, preferred_element_type=jnp.float32)
    grad_keys = (
        lead_dot(grad_edge_scores, edge_queries)
        .reshape(blocks, BLK, DH)
        .at[block_list]
        .add(grad_near_keys)
    )
    grad_values = (
        lead_dot(edge_low, grad_edge).reshape(blocks, BLK, DH).at[block_list].add(grad_near_values)
    )
    grad_queries = jnp.concatenate(
        [grad_query_edge[:BLK], grad_query_mid.reshape(-1, DH), grad_query_edge[BLK:]], axis=0
    )
    return jnp.stack(
        [grad_queries, grad_keys.reshape(-1, DH), grad_values.reshape(-1, DH)], axis=0
    ).astype(jnp.bfloat16)


def per_device(
    tokens,
    segment_ids,
    random_blocks,
    ln1_gain,
    ln1_bias,
    w_qkv,
    w_out,
    ln2_gain,
    ln2_bias,
    w_in,
    b_in,
    w_down,
    b_down,
    cotangent,
):
    gain_one, bias_one, qkv_weight, out_weight = (
        lax.all_gather(ln1_gain, "fsdp", axis=0, tiled=True),
        lax.all_gather(ln1_bias, "fsdp", axis=0, tiled=True),
        lax.all_gather(w_qkv, "fsdp", axis=0, tiled=True),
        lax.all_gather(w_out, "fsdp", axis=0, tiled=True),
    )
    gain_two, bias_two, in_weight, in_bias, down_weight, down_bias = (
        lax.all_gather(ln2_gain, "fsdp", axis=0, tiled=True),
        lax.all_gather(ln2_bias, "fsdp", axis=0, tiled=True),
        lax.all_gather(w_in, "fsdp", axis=0, tiled=True),
        lax.all_gather(b_in, "fsdp", axis=0, tiled=True),
        lax.all_gather(w_down, "fsdp", axis=0, tiled=True),
        lax.all_gather(b_down, "fsdp", axis=0, tiled=True),
    )
    token_rows = tokens[0].astype(jnp.float32)
    tok_count, width = token_rows.shape
    norm_one, pull_one = jax.vjp(
        layer_norm, token_rows, gain_one.astype(jnp.float32), bias_one.astype(jnp.float32)
    )
    normed_one = norm_one.astype(jnp.bfloat16)
    qkv_rows = (
        jnp.dot(normed_one, qkv_weight, preferred_element_type=jnp.float32)
        .astype(jnp.bfloat16)
        .reshape(tok_count, 3, width)
    )
    by_heads = lax.all_to_all(qkv_rows, "seq", split_axis=2, concat_axis=0, tiled=True)
    seq_ids = lax.all_gather(segment_ids[0], "seq", axis=0, tiled=True)
    length = by_heads.shape[0]
    head_count = random_blocks.shape[0]
    head_split = by_heads.reshape(length, 3, head_count, DH).transpose(1, 2, 0, 3)
    block_list, usable = build_lists(random_blocks, length // BLK)

    def forward_head(operands):
        return head_forward(operands[0], operands[1], operands[2], operands[3], usable, seq_ids)

    head_out, log_mid, log_edge = lax.map(
        forward_head, (head_split[0], head_split[1], head_split[2], block_list)
    )
    att_heads = head_out.transpose(1, 0, 2).reshape(length, head_count * DH).astype(jnp.bfloat16)
    att_rows = lax.all_to_all(att_heads, "seq", split_axis=0, concat_axis=1, tiled=True)
    branch = jnp.dot(att_rows, out_weight, preferred_element_type=jnp.float32)
    hidden = token_rows + branch
    norm_two, pull_two = jax.vjp(
        layer_norm, hidden, gain_two.astype(jnp.float32), bias_two.astype(jnp.float32)
    )
    normed_two = norm_two.astype(jnp.bfloat16)
    pre_act = jnp.dot(normed_two, in_weight, preferred_element_type=jnp.float32) + in_bias.astype(
        jnp.float32
    )
    act_value, pull_gelu = jax.vjp(gelu_tanh, pre_act)
    act_low = act_value.astype(jnp.bfloat16)
    result = (
        hidden
        + jnp.dot(act_low, down_weight, preferred_element_type=jnp.float32)
        + down_bias.astype(jnp.float32)
    )
    cot_low = cotangent[0]
    cot_rows = cot_low.astype(jnp.float32)
    in_back, down_back = (
        lax.all_gather(w_in, "fsdp", axis=0, tiled=True),
        lax.all_gather(w_down, "fsdp", axis=0, tiled=True),
    )
    grad_down = lead_dot(act_low, cot_low)
    grad_down_bias = jnp.sum(cot_rows, axis=0)
    grad_act = last_dot(cot_low, down_back)
    grad_pre = pull_gelu(grad_act)[0].astype(jnp.bfloat16)
    grad_in = lead_dot(normed_two, grad_pre)
    grad_in_bias = jnp.sum(grad_pre.astype(jnp.float32), axis=0)
    grad_norm_two = last_dot(grad_pre, in_back)
    grad_hidden_norm, grad_gain_two, grad_bias_two = pull_two(grad_norm_two)
    grad_hidden = cot_rows + grad_hidden_norm
    ffn_shares = (
        lax.psum_scatter(grad_gain_two, "fsdp", scatter_dimension=0, tiled=True),
        lax.psum_scatter(grad_bias_two, "fsdp", scatter_dimension=0, tiled=True),
        lax.psum_scatter(grad_in, "fsdp", scatter_dimension=0, tiled=True),
        lax.psum_scatter(grad_in_bias, "fsdp", scatter_dimension=0, tiled=True),
        lax.psum_scatter(grad_down, "fsdp", scatter_dimension=0, tiled=True),
        lax.psum_scatter(grad_down_bias, "fsdp", scatter_dimension=0, tiled=True),
    )
    qkv_back, out_back = (
        lax.all_gather(w_qkv, "fsdp", axis=0, tiled=True),
        lax.all_gather(w_out, "fsdp", axis=0, tiled=True),
    )
    hidden_low = grad_hidden.astype(jnp.bfloat16)
    grad_out_proj = lead_dot(att_rows, hidden_low)
    grad_att = last_dot(hidden_low, out_back).astype(jnp.bfloat16)
    grad_att_heads = lax.all_to_all(grad_att, "seq", split_axis=1, concat_axis=0, tiled=True)
    grad_split = grad_att_heads.reshape(length, head_count, DH).transpose(1, 0, 2)

    def backward_head(operands):
        return head_backward(
            operands[0],
            operands[1],
            operands[2],
            operands[3],
            operands[4],
            operands[5],
            operands[6],
            usable,
            seq_ids,
        )

    head_grads = lax.map(
        backward_head,
        (head_split[0], head_split[1], head_split[2], block_list, log_mid, log_edge, grad_split),
    )
    grad_heads = head_grads.transpose(2, 1, 0, 3).reshape(length, 3, head_count * DH)
    grad_qkv_rows = lax.all_to_all(
        grad_heads, "seq", split_axis=0, concat_axis=2, tiled=True
    ).reshape(tok_count, 3 * width)
    grad_qkv = lead_dot(normed_one, grad_qkv_rows)
    grad_norm_one = last_dot(grad_qkv_rows, qkv_back)
    grad_rows_norm, grad_gain_one, grad_bias_one = pull_one(grad_norm_one)
    grad_tokens = (grad_hidden + grad_rows_norm).astype(jnp.bfloat16)[None]
    attn_shares = (
        lax.psum_scatter(grad_gain_one, "fsdp", scatter_dimension=0, tiled=True),
        lax.psum_scatter(grad_bias_one, "fsdp", scatter_dimension=0, tiled=True),
        lax.psum_scatter(grad_qkv, "fsdp", scatter_dimension=0, tiled=True),
        lax.psum_scatter(grad_out_proj, "fsdp", scatter_dimension=0, tiled=True),
    )
    shares = attn_shares + ffn_shares
    totals = lax.psum(
        (
            shares[0],
            shares[1],
            shares[2],
            shares[3],
            shares[4],
            shares[5],
            shares[6],
            shares[7],
            shares[8],
            shares[9],
        ),
        "seq",
    )
    return (
        result.astype(jnp.bfloat16)[None],
        grad_tokens,
        totals[0],
        totals[1],
        totals[2],
        totals[3],
        totals[4],
        totals[5],
        totals[6],
        totals[7],
        totals[8],
        totals[9],
    )


def solution(mesh):
    return jax.shard_map(
        per_device,
        mesh=mesh,
        in_specs=(
            P("fsdp", "seq", None),
            P("fsdp", "seq"),
            P("seq", None, None),
            P("fsdp"),
            P("fsdp"),
            P("fsdp", None),
            P("fsdp", None),
            P("fsdp"),
            P("fsdp"),
            P("fsdp", None),
            P("fsdp"),
            P("fsdp", None),
            P("fsdp"),
            P("fsdp", "seq", None),
        ),
        out_specs=(
            P("fsdp", "seq", None),
            P("fsdp", "seq", None),
            P("fsdp"),
            P("fsdp"),
            P("fsdp", None),
            P("fsdp", None),
            P("fsdp"),
            P("fsdp"),
            P("fsdp", None),
            P("fsdp"),
            P("fsdp", None),
            P("fsdp"),
        ),
        check_vma=False,
    )
```

profile of v0, /device:TPU:0, one launch (start us, length us, event | category | flops | bytes accessed | tf_op | source)
XLA Modules:
  0.0 1317.8 jit_solution(9193868924157783332)
XLA Ops:
  9.4 13.5 %all-gather.1 = bf16[8,1,128]{2,1,0:T(2,128)(2,1)S(1)} all-gather(bf16[1,1,128]{2,1,0:T(2,128)(2,1)} %bitcast.348), channel_id=1, replica_groups=mesh['seq'=4,'fsdp'=8] {'fsdp'}, dimensions={0}, use_global_device_ids=true | all-gather | bytes 2304 | tf_op jit(solution)/shard_map/all_gather | solution.py:199
  23.0 8.8 all-gather.2
  34.1 43.1 %all-gather.12.cloned.1.call-done = bf16[1024,3072]{1,0:T(8,128)(2,1)} async-done(((bf16[128,3072]{1,0:T(8,128)(2,1)}), bf16[1024,3072]{1,0:T(8,128)(2,1)}) %all-gather.12.cloned.1.call-update) | async-done | bytes 6291472 | tf_op jit(solution)/shard_map/all_gather | solution.py:201
  95.5 39.0 %all-gather = s32[1,1536]{1,0:T(1,128)S(1)} all-gather(s32[1,384]{1,0:T(1,128)S(1)} %copy-done.53), channel_id=2, replica_groups=mesh['seq'=4,'fsdp'=8] {'seq'}, dimensions={1}, use_global_device_ids=true | all-gather | bytes 7680 | tf_op jit(solution)/shard_map/all_gather | solution.py:224
  149.5 64.8 %while.26 = (s32[]{:T(128)}, bf16[4,1536,64]{2,1,0:T(8,128)(2,1)}, f32[4,22,64,1]{2,1,3,0:T(8,128)}, f32[4,128,1]{1,2,0:T(1,128)}, s32[128]{0:T(128)S(1)}, /*ind...) while((s32[]{:T(128)}, bf16[4,1536,64]{2,1,0:T(8,128)(2,1)}, ...), condition=%wide.region_7.8_spmd, body=%wide.region_2.7_spmd.sunk | while | flops 243564560 | bytes 28432796 | solution.py:233
  220.7 9.3 all-gather.3
  230.1 10.3 all-gather.4
  240.4 12.9 all-gather.5
  256.4 9.3 convolution_add_fusion
  271.9 11.9 convert_reduce_fusion
  309.3 333.9 %while.27 = (s32[]{:T(128)}, bf16[4,3,1536,64]{2,3,0,1:T(8,128)(2,1)}, s32[128]{0:T(128)S(1)}, s32[1536]{0:T(1024)S(1)}, bf16[4,1536,64]{2,1,0:T(8,128)(2,1)}, /...) while((s32[]{:T(128)}, ...), condition=%wide.region_17.18_spmd, body=%wide.region_12.17_spmd.sunk | while | flops 603952256 | bytes 75161568 | solution.py:300
  340.6 8.3 fusion.198
  348.9 18.4 %scatter_fusion.1 = f32[24,64,64]{2,1,0:T(8,128)S(1)} fusion(f32[24,64,64]{2,1,0:T(8,128)S(1)} %bitcast.297, s32[176]{0:T(256)S(1)} %reshape.627, f32[176,64,64]{2,1,0:T(8,128)} %bitcast.303), kind=kCustom, calls=%fused_computation.6.clone.1 | custom fusion | flops 720896 | bytes 8651456 | tf_op jit(solution)/shard_map/while/body/eval_jaxpr/scatter-add | solution.py:169
  372.6 18.4 %scatter_fusion = f32[24,64,64]{2,1,0:T(8,128)S(1)} fusion(f32[24,64,64]{2,1,0:T(8,128)S(1)} %bitcast.296, s32[176]{0:T(256)S(1)} %reshape.627, f32[176,64,64]{2,1,0:T(8,128)} %bitcast.302), kind=kCustom, calls=%fused_computation.7.clone.1 | custom fusion | flops 720896 | bytes 8651456 | tf_op jit(solution)/shard_map/while/body/eval_jaxpr/scatter-add | solution.py:172
  424.1 8.3 fusion.198
  432.3 18.4 %scatter_fusion.1 = f32[24,64,64]{2,1,0:T(8,128)S(1)} fusion(f32[24,64,64]{2,1,0:T(8,128)S(1)} %bitcast.297, s32[176]{0:T(256)S(1)} %reshape.627, f32[176,64,64]{2,1,0:T(8,128)} %bitcast.303), kind=kCustom, calls=%fused_computation.6.clone.1 | custom fusion | flops 720896 | bytes 8651456 | tf_op jit(solution)/shard_map/while/body/eval_jaxpr/scatter-add | solution.py:169
  456.1 18.4 %scatter_fusion = f32[24,64,64]{2,1,0:T(8,128)S(1)} fusion(f32[24,64,64]{2,1,0:T(8,128)S(1)} %bitcast.296, s32[176]{0:T(256)S(1)} %reshape.627, f32[176,64,64]{2,1,0:T(8,128)} %bitcast.302), kind=kCustom, calls=%fused_computation.7.clone.1 | custom fusion | flops 720896 | bytes 8651456 | tf_op jit(solution)/shard_map/while/body/eval_jaxpr/scatter-add | solution.py:172
  515.8 18.4 %scatter_fusion.1 = f32[24,64,64]{2,1,0:T(8,128)S(1)} fusion(f32[24,64,64]{2,1,0:T(8,128)S(1)} %bitcast.297, s32[176]{0:T(256)S(1)} %reshape.627, f32[176,64,64]{2,1,0:T(8,128)} %bitcast.303), kind=kCustom, calls=%fused_computation.6.clone.1 | custom fusion | flops 720896 | bytes 8651456 | tf_op jit(solution)/shard_map/while/body/eval_jaxpr/scatter-add | solution.py:169
  539.6 18.4 %scatter_fusion = f32[24,64,64]{2,1,0:T(8,128)S(1)} fusion(f32[24,64,64]{2,1,0:T(8,128)S(1)} %bitcast.296, s32[176]{0:T(256)S(1)} %reshape.627, f32[176,64,64]{2,1,0:T(8,128)} %bitcast.302), kind=kCustom, calls=%fused_computation.7.clone.1 | custom fusion | flops 720896 | bytes 8651456 | tf_op jit(solution)/shard_map/while/body/eval_jaxpr/scatter-add | solution.py:172
  599.3 18.4 %scatter_fusion.1 = f32[24,64,64]{2,1,0:T(8,128)S(1)} fusion(f32[24,64,64]{2,1,0:T(8,128)S(1)} %bitcast.297, s32[176]{0:T(256)S(1)} %reshape.627, f32[176,64,64]{2,1,0:T(8,128)} %bitcast.303), kind=kCustom, calls=%fused_computation.6.clone.1 | custom fusion | flops 720896 | bytes 8651456 | tf_op jit(solution)/shard_map/while/body/eval_jaxpr/scatter-add | solution.py:169
  623.0 18.4 %scatter_fusion = f32[24,64,64]{2,1,0:T(8,128)S(1)} fusion(f32[24,64,64]{2,1,0:T(8,128)S(1)} %bitcast.296, s32[176]{0:T(256)S(1)} %reshape.627, f32[176,64,64]{2,1,0:T(8,128)} %bitcast.302), kind=kCustom, calls=%fused_computation.7.clone.1 | custom fusion | flops 720896 | bytes 8651456 | tf_op jit(solution)/shard_map/while/body/eval_jaxpr/scatter-add | solution.py:172
  647.5 38.9 %all_to_all.62 = bf16[1536,3,256]{2,1,0:T(4,128)(2,1)S(1)} all-to-all(bf16[1536,3,256]{2,1,0:T(4,128)(2,1)S(1)} %copy.189), channel_id=1, replica_groups=mesh['seq'=4,'fsdp'=8] {'seq'}, dimensions={0} | all-to-all | bytes 4718592 | tf_op jit(solution)/shard_map/all_to_all | solution.py:305
  699.3 12.3 fusion.78
  713.0 10.2 fusion.95
  723.3 101.4 %reduce-scatter.5.cloned.1.call-done = f32[128,3072]{1,0:T(8,128)} async-done(((f32[1024,3072]{1,0:T(8,128)}), f32[128,3072]{1,0:T(8,128)}) %reduce-scatter.5.cloned.1.call-update) | async-done | bytes 1572880 | tf_op jit(solution)/shard_map/reduce_scatter | solution.py:315
  824.7 169.0 %reduce-scatter.11.cloned.1.call-done = f32[512,1024]{1,0:T(8,128)} async-done(((f32[4096,1024]{1,0:T(8,128)}), f32[512,1024]{1,0:T(8,128)}) %reduce-scatter.11.cloned.1.call-update) | async-done | bytes 2097168 | tf_op jit(solution)/shard_map/reduce_scatter | solution.py:274
  993.7 169.0 %reduce-scatter.9.cloned.1.call-done = f32[128,4096]{1,0:T(8,128)} async-done(((f32[1024,4096]{1,0:T(8,128)}), f32[128,4096]{1,0:T(8,128)}) %reduce-scatter.9.cloned.1.call-update) | async-done | bytes 2097168 | tf_op jit(solution)/shard_map/reduce_scatter | solution.py:272
  1165.2 9.3 all-gather.6
  1174.6 10.5 fusion.71
  1193.6 26.7 %all-reduce.6 = (f32[1024]{0:T(1024)S(1)}, f32[1024]{0:T(1024)S(1)}, f32[1024]{0:T(1024)S(1)}, f32[1024]{0:T(1024)S(1)}, f32[4096]{0:T(1024)S(1)}, /*index=5*/f32[1024]{0:T(1024)S(1)}) all-reduce(f32[1024]{0:T(1024)S(1)} %get-tuple-element.315, f32[1024]{0:T(1024)S(1)} %get-tuple-element.318, ...), channel_id=3, replica_groups=mesh['seq'=4,'fsdp'=8] {'fsdp'}, use_global_device_ids=true, to_apply=%region_21.22.clone | all-reduce | flops 9216 | bytes 73728
  1220.7 11.4 all-reduce.7
  1232.1 72.6 %all-reduce.11.cloned.1.call-done = (f32[128,3072]{1,0:T(8,128)}, f32[128,1024]{1,0:T(8,128)}, f32[128,4096]{1,0:T(8,128)}, f32[512,1024]{1,0:T(8,128)}) async-done(((f32[128,3072]{1,0:T(8,128)}, f32[128,1024]{1,0:T(8,128)}, f32[128,4096]{1,0:T(8,128)}, f32[512,1024]{1,0:T(8,128)}), (f32[128,3072]{1,0:T(8,128)}, f32[128,1024]{1,0:T(8,128)}, f32[128,4096]{1,0:T(8,128)}, ...) | async-done | bytes 6291472 | tf_op jit(solution)/shard_map/psum | solution.py:319
  (574 shorter events, 347.3 us)
Async XLA Ops:
  7.2 26.0 %copy-start.2 = (bf16[1,384,1024]{2,1,0:T(8,128)(2,1)S(1)}, bf16[1,384,1024]{2,1,0:T(8,128)(2,1)}, u32[]{:S(2)}) copy-start(bf16[1,384,1024]{2,1,0:T(8,128)(2,1)} %param.18) | copy-start | bytes 2359300
  7.2 70.0 %all-gather.12.cloned.1.call-start = ((), (), s32[]{:S(2)}) async-start(), calls=%async_computation.8 | async-start | bytes 7077888 | tf_op jit(solution)/shard_map/all_gather | solution.py:201
  7.9 245.4 %all-gather.14.cloned.1.call-start = ((), (), s32[]{:S(2)}) async-start(), calls=%async_computation.9 | async-start | bytes 2359296 | tf_op jit(solution)/shard_map/all_gather | solution.py:202
  8.7 247.7 %all-gather.16.cloned.1.call-start = ((), (), s32[]{:S(2)}) async-start(), calls=%async_computation.10 | async-start | bytes 9437184 | tf_op jit(solution)/shard_map/all_gather | solution.py:207
  23.0 54.2 %copy-start.31 = (f32[8,1,128]{2,1,0:T(1,128)}, f32[8,1,128]{2,1,0:T(1,128)S(1)}, u32[]{:S(2)}) copy-start(f32[8,1,128]{2,1,0:T(1,128)S(1)} %convert_element_type.130) | copy-start | bytes 12292
  31.8 45.4 %copy-start.33 = (f32[8,1,128]{2,1,0:T(1,128)}, f32[8,1,128]{2,1,0:T(1,128)S(1)}, u32[]{:S(2)}) copy-start(f32[8,1,128]{2,1,0:T(1,128)S(1)} %convert_element_type.131) | copy-start | bytes 12292
  33.1 44.1 %copy-start.37 = (f32[384]{0:T(512)}, f32[384]{0:T(512)S(1)}, u32[]{:S(2)}) copy-start(f32[384]{0:T(512)S(1)} %broadcast_multiply_fusion.1) | copy-start | bytes 4612
  34.1 43.1 %copy-start.41 = (f32[384]{0:T(512)}, f32[384]{0:T(512)S(1)}, u32[]{:S(2)}) copy-start(f32[384]{0:T(512)S(1)} %fusion.92) | copy-start | bytes 4612
  90.8 43.7 %copy-start.50 = (s32[4,22,3]{1,0,2:T(4,128)S(1)}, s32[4,22,3]{1,0,2:T(4,128)}, u32[]{:S(2)}) copy-start(s32[4,22,3]{1,0,2:T(4,128)} %param.20) | copy-start | bytes 3172
  90.8 43.8 %copy-start.55 = (s32[22,2]{0,1:T(2,128)S(1)}, s32[22,2]{0,1:T(2,128)}, u32[]{:S(2)}) copy-start(s32[22,2]{0,1:T(2,128)} %constant.106.clone.1) | copy-start | bytes 532
  90.8 44.1 %all-to-all-start = ((bf16[384,3,1024]{0,1,2:T(4,128)(2,1)}), bf16[384,3,1024]{0,1,2:T(4,128)(2,1)S(1)}, u32[]{:S(2)}, u32[]{:S(2)}) async-start(bf16[384,3,1024]{0,1,2:T(4,128)(2,1)} %copy.169), calls=%async_computation | async-start | bytes 6291456 | tf_op jit(solution)/shard_map/all_to_all | solution.py:223
  94.6 177.3 %all-gather.18.cloned.1.call-start = ((), (), s32[]{:S(2)}) async-start(), calls=%async_computation.11 | async-start | bytes 9437184 | tf_op jit(solution)/shard_map/all_gather | solution.py:209
  216.0 14.0 %copy-start.57 = (bf16[128]{0:T(256)(128)(2,1)S(1)}, bf16[128]{0:T(256)(128)(2,1)}, u32[]{:S(2)}) copy-start(bf16[128]{0:T(256)(128)(2,1)} %param.26) | copy-start | bytes 772
  216.0 37.3 %copy-start.3 = (bf16[1,384,1024]{2,1,0:T(8,128)(2,1)S(1)}, bf16[1,384,1024]{2,1,0:T(8,128)(2,1)}, u32[]{:S(2)}) copy-start(bf16[1,384,1024]{2,1,0:T(8,128)(2,1)} %param.18) | copy-start | bytes 2359300
  217.2 36.1 %all-to-all-start.1 = ((bf16[4,384,256]{1,2,0:T(8,128)(2,1)}), bf16[4,384,256]{1,2,0:T(8,128)(2,1)S(1)}, u32[]{:S(2)}, u32[]{:S(2)}) async-start(bf16[4,384,256]{1,2,0:T(8,128)(2,1)} %copy.179), calls=%async_computation.1 | async-start | bytes 1572864 | tf_op jit(solution)/shard_map/all_to_all | solution.py:237
  230.1 58.1 %copy-start.22 = (f32[8,1,128]{2,1,0:T(1,128)}, f32[8,1,128]{2,1,0:T(1,128)S(1)}, u32[]{:S(2)}) copy-start(f32[8,1,128]{2,1,0:T(1,128)S(1)} %convert_element_type.132) | copy-start | bytes 12292
  240.3 16.0 %copy-start.26 = (f32[8,1,128]{2,1,0:T(1,128)}, f32[8,1,128]{2,1,0:T(1,128)S(1)}, u32[]{:S(2)}) copy-start(f32[8,1,128]{2,1,0:T(1,128)S(1)} %convert_element_type.133) | copy-start | bytes 12292
  256.0 32.2 %copy-start.5 = (f32[384,1024]{1,0:T(8,128)}, f32[384,1024]{1,0:T(8,128)S(1)}, u32[]{:S(2)}) copy-start(f32[384,1024]{1,0:T(8,128)S(1)} %get-tuple-element.416) | copy-start | bytes 4718596
  256.0 32.2 %copy-start.35 = (f32[384]{0:T(512)}, f32[384]{0:T(512)S(1)}, u32[]{:S(2)}) copy-start(f32[384]{0:T(512)S(1)} %broadcast_multiply_fusion) | copy-start | bytes 4612
  256.3 31.9 %copy-start.39 = (f32[384]{0:T(512)}, f32[384]{0:T(512)S(1)}, u32[]{:S(2)}) copy-start(f32[384]{0:T(512)S(1)} %fusion.93) | copy-start | bytes 4612
  256.4 15.6 %copy-start.12 = (bf16[1,384,1024]{2,1,0:T(8,128)(2,1)S(1)}, bf16[1,384,1024]{2,1,0:T(8,128)(2,1)}, u32[]{:S(2)}) copy-start(bf16[1,384,1024]{2,1,0:T(8,128)(2,1)} %param.31) | copy-start | bytes 2359300
  271.9 11.9 copy-start.59
  292.6 15.0 %all-to-all-start.2 = ((bf16[384,4,256]{0,2,1:T(8,128)(2,1)}), bf16[384,4,256]{0,2,1:T(8,128)(2,1)S(1)}, u32[]{:S(2)}, u32[]{:S(2)}) async-start(bf16[384,4,256]{0,2,1:T(8,128)(2,1)} %bitcast.63), calls=%async_computation.2 | async-start | bytes 1572864 | tf_op jit(solution)/shard_map/all_to_all | solution.py:284
  296.3 427.0 %reduce-scatter.7.cloned.1.call-start = ((), (), s32[]{:S(2)}) async-start(), calls=%async_computation.13 | async-start | bytes 4718592 | tf_op jit(solution)/shard_map/reduce_scatter | solution.py:316
  299.5 525.2 %reduce-scatter.5.cloned.1.call-start = ((), (), s32[]{:S(2)}) async-start(), calls=%async_computation.12 | async-start | bytes 14155776 | tf_op jit(solution)/shard_map/reduce_scatter | solution.py:315
  309.4 10.7 copy-start.48
  392.9 10.7 copy-start.48
  476.4 10.7 copy-start.48
  559.8 10.7 copy-start.48
  698.2 295.6 %reduce-scatter.11.cloned.1.call-start = ((), (), s32[]{:S(2)}) async-start(), calls=%async_computation.15 | async-start | bytes 18874368 | tf_op jit(solution)/shard_map/reduce_scatter | solution.py:274
  711.6 451.1 %reduce-scatter.9.cloned.1.call-start = ((), (), s32[]{:S(2)}) async-start(), calls=%async_computation.14 | async-start | bytes 18874368 | tf_op jit(solution)/shard_map/reduce_scatter | solution.py:272
  723.2 581.5 %all-reduce.11.cloned.1.call-start = ((), (), s32[]{:S(2)}) async-start(), calls=%async_computation.16 | async-start | bytes 12582912 | tf_op jit(solution)/shard_map/psum | solution.py:319
  (77 other events, 289.4 us)
Sparse Core Ops, SparseCore 0:
  9.7 67.4 all-gather.11
  78.8 27.6 all-gather.13
  108.1 81.6 all-gather.15
  191.2 80.6 all-gather.17
  299.6 48.9 reduce-scatter.6
  698.3 126.3 reduce-scatter.4
  827.1 166.6 reduce-scatter.10
  996.1 166.5 reduce-scatter.8
  1166.5 138.2 all-reduce.10
where the time goes:
time: 1330 us; the launch traced here: 1320 us
  waiting for transfers between devices  572 us (43%)
  matrix products  213 us (16%)
  blocking collectives  180 us (14%)
  other arithmetic  168 us (13%)
  local copies, waits for them, and re-layouts  156 us (12%)
  between operations  16 us (1%)
    reduce_scatter x1, waiting for transfers between devices, per_device(): lax.psum_scatter(grad_down, 'fsdp', scatter_dimension=0, tiled=True)  169 us
    reduce_scatter x1, waiting for transfers between devices, per_device(): lax.psum_scatter(grad_in, 'fsdp', scatter_dimension=0, tiled=True)  169 us
    reduce_scatter x1, waiting for transfers between devices, per_device(): lax.psum_scatter(grad_qkv, 'fsdp', scatter_dimension=0, tiled=True)  101 us
    scatter-add x4, other arithmetic, head_backward(): grad_keys = lead_dot(grad_edge_scores, edge_queries).reshape(blocks, BLK,...  73.5 us
    scatter-add x4, other arithmetic, head_backward(): lead_dot(edge_low, grad_edge).reshape(blocks, BLK, DH).at[block_list]  73.5 us
    psum x1, waiting for transfers between devices, per_device(): lax.psum((shares[0], shares[1], shares[2], shares[3], shares[4], shares[5...  72.6 us
    all_gather x1, waiting for transfers between devices, per_device(): lax.all_gather(w_qkv, 'fsdp', axis=0, tiled=True)  43.1 us
    all_gather x1, blocking collectives, per_device(): seq_ids = lax.all_gather(segment_ids[0], 'seq', axis=0, tiled=True)  39 us
  transfers between devices with their start and end apart: 12, of which 7 were waited for; matrix products, arithmetic and copies ran while one was open for 38% of the time, Pallas kernels for 0%

commit v1 on v0

--- a/solution.py
+++ b/solution.py
@@ -221,7 +221,21 @@
         .reshape(tok_count, 3, width)
     )
     by_heads = lax.all_to_all(qkv_rows, "seq", split_axis=2, concat_axis=0, tiled=True)
-    seq_ids = lax.all_gather(segment_ids[0], "seq", axis=0, tiled=True)
+
+    def lift_joints(unit):
+        q_n = lax.psum(1, "seq")
+        top = sorted(((idx, (idx + 1) % q_n) for idx in range(q_n)))
+        x_now = unit
+        found = [x_now]
+        for i in range(1, q_n):
+            x_now = lax.ppermute(x_now, "seq", top)
+            found.insert(0, x_now)
+        piece_now = jnp.concatenate(found, axis=0)
+        mat_out = lax.axis_index("seq")
+        block_next = mat_out + 1
+        return jnp.roll(piece_now, shift=block_next * unit.shape[0], axis=0)
+
+    seq_ids = lift_joints(segment_ids[0])
     length = by_heads.shape[0]
     head_count = random_blocks.shape[0]
     head_split = by_heads.reshape(length, 3, head_count, DH).transpose(1, 2, 0, 3)

time: 1330 us -> 1330 us (level)
  blocking collectives: 180 us -> 141 us
  waiting for transfers between devices: 572 us -> 606 us
    ppermute x0 -> x3, waiting for transfers between devices: none -> 39.7 us  [lift_joints(): x_now = lax.ppermute(x_now, 'seq', top)]
    all_gather x1 -> x0, blocking collectives: 39 us -> none  [per_device(): seq_ids = lax.all_gather(segment_ids[0], 'seq', axis=0, tiled=True)]
  transfers between devices with their start and end apart: 12 -> 15, of which waited for: 7 -> 9; matrix products, arithmetic and copies ran while one was open for 38% -> 38% of each run, Pallas kernels for 0% -> 0%
where the time goes in v1:
time: 1330 us; the launch traced here: 1320 us
  waiting for transfers between devices  606 us (46%)
  matrix products  213 us (16%)
  other arithmetic  167 us (13%)
  local copies, waits for them, and re-layouts  156 us (12%)
  blocking collectives  141 us (11%)
  starting transfers between devices  16.9 us (1%)
  between operations  16.1 us (1%)
    reduce_scatter x1, waiting for transfers between devices, per_device(): lax.psum_scatter(grad_down, 'fsdp', scatter_dimension=0, tiled=True)  169 us
    reduce_scatter x1, waiting for transfers between devices, per_device(): lax.psum_scatter(grad_in, 'fsdp', scatter_dimension=0, tiled=True)  169 us
    reduce_scatter x1, waiting for transfers between devices, per_device(): lax.psum_scatter(grad_qkv, 'fsdp', scatter_dimension=0, tiled=True)  101 us
    scatter-add x4, other arithmetic, head_backward(): grad_keys = lead_dot(grad_edge_scores, edge_queries).reshape(blocks, BLK,...  73.5 us
    scatter-add x4, other arithmetic, head_backward(): lead_dot(edge_low, grad_edge).reshape(blocks, BLK, DH).at[block_list]  73.5 us
    psum x1, waiting for transfers between devices, per_device(): lax.psum((shares[0], shares[1], shares[2], shares[3], shares[4], shares[5...  72.6 us
    all_gather x1, waiting for transfers between devices, per_device(): lax.all_gather(w_qkv, 'fsdp', axis=0, tiled=True)  42 us
    ppermute x3, waiting for transfers between devices, lift_joints(): x_now = lax.ppermute(x_now, 'seq', top)  39.7 us
  transfers between devices with their start and end apart: 15, of which 9 were waited for; matrix products, arithmetic and copies ran while one was open for 38% of the time, Pallas kernels for 0%

profile of v1, /device:TPU:0, one launch (start us, length us, event | category | flops | bytes accessed | tf_op | source)
XLA Modules:
  0.0 1317.7 jit_solution(15591807896573445334)
XLA Ops:
  14.3 12.0 all-gather
  26.4 8.8 all-gather.1
  35.2 42.0 %all-gather.11.cloned.1.call-done = bf16[1024,3072]{1,0:T(8,128)(2,1)} async-done(((bf16[128,3072]{1,0:T(8,128)(2,1)}), bf16[1024,3072]{1,0:T(8,128)(2,1)}) %all-gather.11.cloned.1.call-update) | async-done | bytes 6291472 | tf_op jit(solution)/shard_map/all_gather | solution.py:201
  96.8 35.6 %collective-permute-done.1 = s32[384]{0:T(512)S(1)} collective-permute-done((s32[384]{0:T(512)S(1)}, s32[384]{0:T(512)S(1)}, u32[]{:S(2)}, u32[]{:S(2)}) %collective-permute-start.1) | collective-permute-done | bytes 1568 | tf_op jit(solution)/shard_map/ppermute | solution.py:231
  152.0 64.9 %while.26 = (s32[]{:T(128)}, bf16[4,1536,64]{2,1,0:T(8,128)(2,1)}, f32[4,22,64,1]{2,1,3,0:T(8,128)}, f32[4,128,1]{1,2,0:T(1,128)}, s32[128]{0:T(128)S(1)}, /*ind...) while((s32[]{:T(128)}, bf16[4,1536,64]{2,1,0:T(8,128)(2,1)}, ...), condition=%wide.region_7.8_spmd, body=%wide.region_2.7_spmd.sunk | while | flops 243564560 | bytes 28432796 | solution.py:247
  223.3 8.9 all-gather.2
  232.2 10.0 all-gather.3
  242.2 14.4 %all-gather.4 = bf16[8,1,512]{2,1,0:T(2,128)(2,1)S(1)} all-gather(bf16[1,1,512]{2,1,0:T(2,128)(2,1)S(1)} %reshape.569), channel_id=1, replica_groups=mesh['seq'=4,'fsdp'=8] {'fsdp'}, dimensions={0}, use_global_device_ids=true | all-gather | bytes 9216 | tf_op jit(solution)/shard_map/all_gather | solution.py:208
  259.8 9.3 convolution_add_fusion
  272.1 11.9 convert_reduce_fusion
  309.5 333.8 %while.27 = (s32[]{:T(128)}, bf16[4,3,1536,64]{2,3,0,1:T(8,128)(2,1)}, s32[128]{0:T(128)S(1)}, s32[1536]{0:T(1024)S(1)}, bf16[4,1536,64]{2,1,0:T(8,128)(2,1)}, /...) while((s32[]{:T(128)}, ...), condition=%wide.region_17.18_spmd, body=%wide.region_12.17_spmd.sunk | while | flops 603952256 | bytes 75161568 | solution.py:314
  340.7 8.2 fusion.199
  349.0 18.4 %scatter_fusion.1 = f32[24,64,64]{2,1,0:T(8,128)S(1)} fusion(f32[24,64,64]{2,1,0:T(8,128)S(1)} %bitcast.293, s32[176]{0:T(256)S(1)} %reshape.624, f32[176,64,64]{2,1,0:T(8,128)} %bitcast.299), kind=kCustom, calls=%fused_computation.6.clone.1 | custom fusion | flops 720896 | bytes 8651456 | tf_op jit(solution)/shard_map/while/body/eval_jaxpr/scatter-add | solution.py:169
  372.7 18.4 %scatter_fusion = f32[24,64,64]{2,1,0:T(8,128)S(1)} fusion(f32[24,64,64]{2,1,0:T(8,128)S(1)} %bitcast.292, s32[176]{0:T(256)S(1)} %reshape.624, f32[176,64,64]{2,1,0:T(8,128)} %bitcast.298), kind=kCustom, calls=%fused_computation.7.clone.1 | custom fusion | flops 720896 | bytes 8651456 | tf_op jit(solution)/shard_map/while/body/eval_jaxpr/scatter-add | solution.py:172
  424.2 8.2 fusion.199
  432.4 18.4 %scatter_fusion.1 = f32[24,64,64]{2,1,0:T(8,128)S(1)} fusion(f32[24,64,64]{2,1,0:T(8,128)S(1)} %bitcast.293, s32[176]{0:T(256)S(1)} %reshape.624, f32[176,64,64]{2,1,0:T(8,128)} %bitcast.299), kind=kCustom, calls=%fused_computation.6.clone.1 | custom fusion | flops 720896 | bytes 8651456 | tf_op jit(solution)/shard_map/while/body/eval_jaxpr/scatter-add | solution.py:169
  456.2 18.4 %scatter_fusion = f32[24,64,64]{2,1,0:T(8,128)S(1)} fusion(f32[24,64,64]{2,1,0:T(8,128)S(1)} %bitcast.292, s32[176]{0:T(256)S(1)} %reshape.624, f32[176,64,64]{2,1,0:T(8,128)} %bitcast.298), kind=kCustom, calls=%fused_computation.7.clone.1 | custom fusion | flops 720896 | bytes 8651456 | tf_op jit(solution)/shard_map/while/body/eval_jaxpr/scatter-add | solution.py:172
  515.8 18.4 %scatter_fusion.1 = f32[24,64,64]{2,1,0:T(8,128)S(1)} fusion(f32[24,64,64]{2,1,0:T(8,128)S(1)} %bitcast.293, s32[176]{0:T(256)S(1)} %reshape.624, f32[176,64,64]{2,1,0:T(8,128)} %bitcast.299), kind=kCustom, calls=%fused_computation.6.clone.1 | custom fusion | flops 720896 | bytes 8651456 | tf_op jit(solution)/shard_map/while/body/eval_jaxpr/scatter-add | solution.py:169
  539.6 18.4 %scatter_fusion = f32[24,64,64]{2,1,0:T(8,128)S(1)} fusion(f32[24,64,64]{2,1,0:T(8,128)S(1)} %bitcast.292, s32[176]{0:T(256)S(1)} %reshape.624, f32[176,64,64]{2,1,0:T(8,128)} %bitcast.298), kind=kCustom, calls=%fused_computation.7.clone.1 | custom fusion | flops 720896 | bytes 8651456 | tf_op jit(solution)/shard_map/while/body/eval_jaxpr/scatter-add | solution.py:172
  599.2 18.4 %scatter_fusion.1 = f32[24,64,64]{2,1,0:T(8,128)S(1)} fusion(f32[24,64,64]{2,1,0:T(8,128)S(1)} %bitcast.293, s32[176]{0:T(256)S(1)} %reshape.624, f32[176,64,64]{2,1,0:T(8,128)} %bitcast.299), kind=kCustom, calls=%fused_computation.6.clone.1 | custom fusion | flops 720896 | bytes 8651456 | tf_op jit(solution)/shard_map/while/body/eval_jaxpr/scatter-add | solution.py:169
  623.0 18.4 %scatter_fusion = f32[24,64,64]{2,1,0:T(8,128)S(1)} fusion(f32[24,64,64]{2,1,0:T(8,128)S(1)} %bitcast.292, s32[176]{0:T(256)S(1)} %reshape.624, f32[176,64,64]{2,1,0:T(8,128)} %bitcast.298), kind=kCustom, calls=%fused_computation.7.clone.1 | custom fusion | flops 720896 | bytes 8651456 | tf_op jit(solution)/shard_map/while/body/eval_jaxpr/scatter-add | solution.py:172
  647.5 38.9 %all_to_all.62 = bf16[1536,3,256]{2,1,0:T(4,128)(2,1)S(1)} all-to-all(bf16[1536,3,256]{2,1,0:T(4,128)(2,1)S(1)} %copy.189), channel_id=1, replica_groups=mesh['seq'=4,'fsdp'=8] {'seq'}, dimensions={0} | all-to-all | bytes 4718592 | tf_op jit(solution)/shard_map/all_to_all | solution.py:319
  699.3 12.4 fusion.78
  713.1 10.2 fusion.95
  723.3 101.3 %reduce-scatter.5.cloned.1.call-done = f32[128,3072]{1,0:T(8,128)} async-done(((f32[1024,3072]{1,0:T(8,128)}), f32[128,3072]{1,0:T(8,128)}) %reduce-scatter.5.cloned.1.call-update) | async-done | bytes 1572880 | tf_op jit(solution)/shard_map/reduce_scatter | solution.py:329
  824.7 169.0 %reduce-scatter.11.cloned.1.call-done = f32[512,1024]{1,0:T(8,128)} async-done(((f32[4096,1024]{1,0:T(8,128)}), f32[512,1024]{1,0:T(8,128)}) %reduce-scatter.11.cloned.1.call-update) | async-done | bytes 2097168 | tf_op jit(solution)/shard_map/reduce_scatter | solution.py:288
  993.6 169.0 %reduce-scatter.9.cloned.1.call-done = f32[128,4096]{1,0:T(8,128)} async-done(((f32[1024,4096]{1,0:T(8,128)}), f32[128,4096]{1,0:T(8,128)}) %reduce-scatter.9.cloned.1.call-update) | async-done | bytes 2097168 | tf_op jit(solution)/shard_map/reduce_scatter | solution.py:286
  1165.2 9.3 all-gather.5
  1174.5 10.5 fusion.71
  1193.4 26.7 %all-reduce.6 = (f32[1024]{0:T(1024)S(1)}, f32[1024]{0:T(1024)S(1)}, f32[1024]{0:T(1024)S(1)}, f32[1024]{0:T(1024)S(1)}, f32[4096]{0:T(1024)S(1)}, /*index=5*/f32[1024]{0:T(1024)S(1)}) all-reduce(f32[1024]{0:T(1024)S(1)} %get-tuple-element.315, f32[1024]{0:T(1024)S(1)} %get-tuple-element.318, ...), channel_id=2, replica_groups=mesh['seq'=4,'fsdp'=8] {'fsdp'}, use_global_device_ids=true, to_apply=%region_21.22.clone | all-reduce | flops 9216 | bytes 73728
  1220.6 11.4 all-reduce.7
  1232.0 72.6 %all-reduce.11.cloned.1.call-done = (f32[128,3072]{1,0:T(8,128)}, f32[128,1024]{1,0:T(8,128)}, f32[128,4096]{1,0:T(8,128)}, f32[512,1024]{1,0:T(8,128)}) async-done(((f32[128,3072]{1,0:T(8,128)}, f32[128,1024]{1,0:T(8,128)}, f32[128,4096]{1,0:T(8,128)}, f32[512,1024]{1,0:T(8,128)}), (f32[128,3072]{1,0:T(8,128)}, f32[128,1024]{1,0:T(8,128)}, f32[128,4096]{1,0:T(8,128)}, ...) | async-done | bytes 6291472 | tf_op jit(solution)/shard_map/psum | solution.py:333
  (591 shorter events, 352.4 us)
Async XLA Ops:
  7.2 19.2 %copy-start.56 = (bf16[128]{0:T(256)(128)(2,1)S(1)}, bf16[128]{0:T(256)(128)(2,1)}, u32[]{:S(2)}) copy-start(bf16[128]{0:T(256)(128)(2,1)} %param.22) | copy-start | bytes 772
  7.2 70.0 %all-gather.11.cloned.1.call-start = ((), (), s32[]{:S(2)}) async-start(), calls=%async_computation.8 | async-start | bytes 7077888 | tf_op jit(solution)/shard_map/all_gather | solution.py:201
  7.9 248.8 %all-gather.13.cloned.1.call-start = ((), (), s32[]{:S(2)}) async-start(), calls=%async_computation.9 | async-start | bytes 2359296 | tf_op jit(solution)/shard_map/all_gather | solution.py:202
  8.7 251.1 %all-gather.15.cloned.1.call-start = ((), (), s32[]{:S(2)}) async-start(), calls=%async_computation.10 | async-start | bytes 9437184 | tf_op jit(solution)/shard_map/all_gather | solution.py:207
  9.4 262.7 %all-gather.17.cloned.1.call-start = ((), (), s32[]{:S(2)}) async-start(), calls=%async_computation.11 | async-start | bytes 9437184 | tf_op jit(solution)/shard_map/all_gather | solution.py:209
  10.2 84.6 %collective-permute-start = (s32[384]{0:T(512)S(1)}, s32[384]{0:T(512)S(1)}, u32[]{:S(2)}, u32[]{:S(2)}) collective-permute-start(s32[384]{0:T(512)S(1)} %reduce.1), channel_id=1, source_target_pairs={{0,8},{8,16},{16,24},{24,0},{1,9},{9,17},{17,25},{25,1},{2,10},{10... | collective-permute-start | bytes 4616 | tf_op jit(solution)/shard_map/ppermute | solution.py:231
  13.4 63.8 %copy-start.37 = (f32[384]{0:T(512)}, f32[384]{0:T(512)S(1)}, u32[]{:S(2)}) copy-start(f32[384]{0:T(512)S(1)} %broadcast_multiply_fusion.1) | copy-start | bytes 4612
  13.8 63.5 %copy-start.41 = (f32[384]{0:T(512)}, f32[384]{0:T(512)S(1)}, u32[]{:S(2)}) copy-start(f32[384]{0:T(512)S(1)} %fusion.92) | copy-start | bytes 4612
  26.3 50.9 %copy-start.31 = (f32[8,1,128]{2,1,0:T(1,128)}, f32[8,1,128]{2,1,0:T(1,128)S(1)}, u32[]{:S(2)}) copy-start(f32[8,1,128]{2,1,0:T(1,128)S(1)} %convert_element_type.130) | copy-start | bytes 12292
  35.2 42.1 %copy-start.33 = (f32[8,1,128]{2,1,0:T(1,128)}, f32[8,1,128]{2,1,0:T(1,128)S(1)}, u32[]{:S(2)}) copy-start(f32[8,1,128]{2,1,0:T(1,128)S(1)} %convert_element_type.131) | copy-start | bytes 12292
  90.8 41.7 %copy-start.54 = (s32[22,2]{0,1:T(2,128)S(1)}, s32[22,2]{0,1:T(2,128)}, u32[]{:S(2)}) copy-start(s32[22,2]{0,1:T(2,128)} %constant.128.clone.1) | copy-start | bytes 532
  90.8 46.5 %all-to-all-start = ((bf16[384,3,1024]{0,1,2:T(4,128)(2,1)}), bf16[384,3,1024]{0,1,2:T(4,128)(2,1)S(1)}, u32[]{:S(2)}, u32[]{:S(2)}) async-start(bf16[384,3,1024]{0,1,2:T(4,128)(2,1)} %copy.169), calls=%async_computation | async-start | bytes 6291456 | tf_op jit(solution)/shard_map/all_to_all | solution.py:223
  94.7 37.6 %collective-permute-start.1 = (s32[384]{0:T(512)S(1)}, s32[384]{0:T(512)S(1)}, u32[]{:S(2)}, u32[]{:S(2)}) collective-permute-start(s32[384]{0:T(512)S(1)} %collective-permute-done), channel_id=1, source_target_pairs={{0,8},{8,16},{16,24},{24,0},{1,9},{9,17},{17,25},{25,1},{2,10},{10... | collective-permute-start | bytes 4616 | tf_op jit(solution)/shard_map/ppermute | solution.py:231
  132.4 4.6 collective-permute-start.2
  218.5 13.7 %copy-start.58 = (bf16[128]{0:T(256)(128)(2,1)S(1)}, bf16[128]{0:T(256)(128)(2,1)}, u32[]{:S(2)}) copy-start(bf16[128]{0:T(256)(128)(2,1)} %param.26) | copy-start | bytes 772
  218.6 38.2 %copy-start.3 = (bf16[1,384,1024]{2,1,0:T(8,128)(2,1)S(1)}, bf16[1,384,1024]{2,1,0:T(8,128)(2,1)}, u32[]{:S(2)}) copy-start(bf16[1,384,1024]{2,1,0:T(8,128)(2,1)} %param.18) | copy-start | bytes 2359300
  219.7 37.0 %all-to-all-start.1 = ((bf16[4,384,256]{1,2,0:T(8,128)(2,1)}), bf16[4,384,256]{1,2,0:T(8,128)(2,1)S(1)}, u32[]{:S(2)}, u32[]{:S(2)}) async-start(bf16[4,384,256]{1,2,0:T(8,128)(2,1)} %copy.179), calls=%async_computation.1 | async-start | bytes 1572864 | tf_op jit(solution)/shard_map/all_to_all | solution.py:251
  232.2 56.1 %copy-start.22 = (f32[8,1,128]{2,1,0:T(1,128)}, f32[8,1,128]{2,1,0:T(1,128)S(1)}, u32[]{:S(2)}) copy-start(f32[8,1,128]{2,1,0:T(1,128)S(1)} %convert_element_type.132) | copy-start | bytes 12292
  242.2 17.6 %copy-start.26 = (f32[8,1,128]{2,1,0:T(1,128)}, f32[8,1,128]{2,1,0:T(1,128)S(1)}, u32[]{:S(2)}) copy-start(f32[8,1,128]{2,1,0:T(1,128)S(1)} %convert_element_type.133) | copy-start | bytes 12292
  259.4 29.0 %copy-start.5 = (f32[384,1024]{1,0:T(8,128)}, f32[384,1024]{1,0:T(8,128)S(1)}, u32[]{:S(2)}) copy-start(f32[384,1024]{1,0:T(8,128)S(1)} %get-tuple-element.416) | copy-start | bytes 4718596
  259.4 28.9 %copy-start.35 = (f32[384]{0:T(512)}, f32[384]{0:T(512)S(1)}, u32[]{:S(2)}) copy-start(f32[384]{0:T(512)S(1)} %broadcast_multiply_fusion) | copy-start | bytes 4612
  259.7 28.6 %copy-start.39 = (f32[384]{0:T(512)}, f32[384]{0:T(512)S(1)}, u32[]{:S(2)}) copy-start(f32[384]{0:T(512)S(1)} %fusion.93) | copy-start | bytes 4612
  259.8 12.3 copy-start.12
  272.1 11.9 copy-start.60
  292.7 15.0 %all-to-all-start.2 = ((bf16[384,4,256]{0,2,1:T(8,128)(2,1)}), bf16[384,4,256]{0,2,1:T(8,128)(2,1)S(1)}, u32[]{:S(2)}, u32[]{:S(2)}) async-start(bf16[384,4,256]{0,2,1:T(8,128)(2,1)} %bitcast.61), calls=%async_computation.2 | async-start | bytes 1572864 | tf_op jit(solution)/shard_map/all_to_all | solution.py:298
  296.4 427.0 %reduce-scatter.7.cloned.1.call-start = ((), (), s32[]{:S(2)}) async-start(), calls=%async_computation.13 | async-start | bytes 4718592 | tf_op jit(solution)/shard_map/reduce_scatter | solution.py:330
  299.6 525.0 %reduce-scatter.5.cloned.1.call-start = ((), (), s32[]{:S(2)}) async-start(), calls=%async_computation.12 | async-start | bytes 14155776 | tf_op jit(solution)/shard_map/reduce_scatter | solution.py:329
  309.5 10.7 copy-start.48
  393.0 10.7 copy-start.48
  698.1 295.5 %reduce-scatter.11.cloned.1.call-start = ((), (), s32[]{:S(2)}) async-start(), calls=%async_computation.15 | async-start | bytes 18874368 | tf_op jit(solution)/shard_map/reduce_scatter | solution.py:288
  711.7 450.9 %reduce-scatter.9.cloned.1.call-start = ((), (), s32[]{:S(2)}) async-start(), calls=%async_computation.14 | async-start | bytes 18874368 | tf_op jit(solution)/shard_map/reduce_scatter | solution.py:286
  723.3 581.4 %all-reduce.11.cloned.1.call-start = ((), (), s32[]{:S(2)}) async-start(), calls=%async_computation.16 | async-start | bytes 12582912 | tf_op jit(solution)/shard_map/psum | solution.py:333
  (81 other events, 325.5 us)
Sparse Core Ops, SparseCore 0:
  9.7 67.4 all-gather.10
  78.8 27.6 all-gather.12
  108.2 81.6 all-gather.14
  191.3 80.7 all-gather.16
  299.8 49.0 reduce-scatter.6
  698.3 126.3 reduce-scatter.4
  827.0 166.5 reduce-scatter.10
  996.0 166.5 reduce-scatter.8
  1166.4 138.2 all-reduce.10
